TPU v7x, 32 devices: a whole 2x2x4 slice. The times are simulated.
32 devices in a mesh: shard: 4 (over y, core), replica: 8 (over z, x).
Axes of the slice: x: 2, y: 2, z: 4, core: 2. Of those that a mesh axis runs over, the one named last changes fastest.
Arguments:
- tokens: bfloat16 [8, 1024, 1024], P('replica', 'shard'), may hold values from -6 to 6
- cotangent: bfloat16 [8, 1024, 1024], P('replica', 'shard'), may hold values from -6 to 6
- lengths: int32 [8], P('replica'), may hold values from 256 to 1024, as said below
- block_order: int32 [8, 8], P('replica'), may hold values from 0 to 7, as said below
- norm1_gain: bfloat16 [1024], P('shard'), may hold values from 0.099609375 to 1.8984375
- query_weight: bfloat16 [1024, 2048], P('shard'), may hold values from -0.1875 to 0.1875
- key_weight: bfloat16 [1024, 1024], P('shard'), may hold values from -0.1875 to 0.1875
- value_weight: bfloat16 [1024, 1024], P('shard'), may hold values from -0.1875 to 0.1875
- output_weight: bfloat16 [2048, 1024], P('shard'), may hold values from -1.5 to 1.5
- query_gain: bfloat16 [128], P('shard'), may hold values from 0.099609375 to 1.8984375
- key_gain: bfloat16 [128], P('shard'), may hold values from 0.099609375 to 1.8984375
- norm2_gain: bfloat16 [1024], P('shard'), may hold values from 0.099609375 to 1.8984375
- gate_weight: bfloat16 [1024, 3072], P('shard'), may hold values from -0.1875 to 0.1875
- up_weight: bfloat16 [1024, 3072], P('shard'), may hold values from -0.1875 to 0.1875
- down_weight: bfloat16 [3072, 1024], P('shard'), may hold values from -0.109375 to 0.109375
Outputs:
- output: bfloat16 [8, 1024, 1024], P('replica', 'shard')
- input_grad: float32 [8, 1024, 1024], P('replica', 'shard')
- norm1_gain_grad: float32 [1024], P('shard')
- query_weight_grad: float32 [1024, 2048], P('shard')
- key_weight_grad: float32 [1024, 1024], P('shard')
- value_weight_grad: float32 [1024, 1024], P('shard')
- output_weight_grad: float32 [2048, 1024], P('shard')
- query_gain_grad: float32 [128], P('shard')
- key_gain_grad: float32 [128], P('shard')
- norm2_gain_grad: float32 [1024], P('shard')
- gate_weight_grad: float32 [1024, 3072], P('shard')
- up_weight_grad: float32 [1024, 3072], P('shard')
- down_weight_grad: float32 [3072, 1024], P('shard')
Inputs may be any that keep to these rules, and one draw needn't show every extreme that they name: `lengths`: in every group of 1 sequence one has 1024 valid tokens; valid tokens hold positions 0 to length - 1. `block_order`: each row is a permutation of 0 to 7 in which places 2j and 2j + 1 hold blocks that add up to 7.
All inputs are finite; a program needn't handle non-finite values.
Results may differ from a plain program's by a relative error of at most 0.013.
Values may be sent and summed in bfloat16 or wider, within the bound.
A program may use at most 256 MiB of HBM per device.

v0:
```python
import jax
import jax.numpy as jnp
from jax import lax
from jax.sharding import PartitionSpec as P

EPSILON = 1e-06
ROPE_BASE = 1000000.0
BF = jnp.bfloat16
F32 = jnp.float32


def rms_scale(values, gain_vec):
    return (
        values * lax.rsqrt(jnp.mean(values * values, axis=-1, keepdims=True) + EPSILON) * gain_vec
    )


def rotate_half(values, cosine, sine_table):
    middle = values.shape[-1] // 2
    turned = jnp.concatenate([-values[..., middle:], values[..., :middle]], axis=-1)
    return values * cosine + turned * sine_table


def rotary_tables(position, head_width):
    middle = head_width // 2
    exponent = jnp.arange(middle, dtype=F32) * 2.0 / head_width
    inverse = ROPE_BASE ** (-exponent)
    phases = position.astype(F32)[..., None] * inverse
    phases = jnp.concatenate([phases, phases], axis=-1)
    return (jnp.cos(phases), jnp.sin(phases))


def mm(a, b):
    return jnp.einsum("ri,io->ro", a, b, preferred_element_type=F32)


def mm_t(a, b):
    return jnp.einsum("ro,io->ri", a, b, preferred_element_type=F32)


def mm_w(a, b):
    return jnp.einsum("ri,ro->io", a, b, preferred_element_type=F32)


def gather_rows(v):
    return lax.all_gather(v, "shard", axis=0, tiled=True)


def scatter_rows(v):
    return lax.psum_scatter(v.astype(BF), "shard", scatter_dimension=0, tiled=True).astype(F32)


def to_columns(w):
    return lax.all_to_all(w, "shard", split_axis=1, concat_axis=0, tiled=True)


def to_rows(g):
    return lax.all_to_all(g, "shard", split_axis=0, concat_axis=1, tiled=True)


def shards(
    tokens,
    cotangent,
    lengths,
    block_order,
    norm1_gain,
    query_weight,
    key_weight,
    value_weight,
    output_weight,
    query_gain,
    key_gain,
    norm2_gain,
    gate_weight,
    up_weight,
    down_weight,
):
    shard_count = lax.axis_size("shard")
    row_count = tokens.shape[1]
    block_count = block_order.shape[1]
    slot_len = row_count * shard_count
    block_len = slot_len // block_count
    head_width = query_gain.shape[0] * shard_count
    score_scale = head_width ** (-0.5)
    gains = lax.all_gather(
        jnp.concatenate([norm1_gain, norm2_gain, query_gain, key_gain]), "shard", axis=0
    )
    wide = norm1_gain.shape[0]
    gain_one = gains[:, :wide].reshape(-1).astype(F32)
    gain_two = gains[:, wide : 2 * wide].reshape(-1).astype(F32)
    gain_query = gains[:, 2 * wide : 2 * wide + query_gain.shape[0]].reshape(-1).astype(F32)
    gain_key = gains[:, 2 * wide + query_gain.shape[0] :].reshape(-1).astype(F32)
    w_qkv = tuple((to_columns(w) for w in (query_weight, key_weight, value_weight)))
    w_gate, w_up = (to_columns(gate_weight), to_columns(up_weight))
    heads = w_qkv[0].shape[1] // head_width
    kvs = w_qkv[1].shape[1] // head_width
    per = heads // kvs
    offsets = jnp.arange(slot_len, dtype=jnp.int32)
    pos_all = (
        jnp.repeat(block_order[0], block_len, total_repeat_length=slot_len) * block_len
        + offsets % block_len
    )
    pos_local = lax.dynamic_slice_in_dim(pos_all, lax.axis_index("shard") * row_count, row_count)
    valid_rows = (pos_local < lengths[0]).astype(F32)[:, None]
    allowed = pos_all[None, None, None, :] <= pos_all[None, None, :, None]
    inputs = tokens[0].astype(F32)
    normed_f, norm_one_back = jax.vjp(rms_scale, inputs, gain_one)
    normed = gather_rows(normed_f.astype(BF))
    grad_result = cotangent[0].astype(F32) * valid_rows
    grad_branch = gather_rows(grad_result.astype(BF))
    query_raw = mm(normed, w_qkv[0]).reshape(slot_len, heads, head_width)
    key_raw = mm(normed, w_qkv[1]).reshape(slot_len, kvs, head_width)
    value = mm(normed, w_qkv[2]).astype(BF).reshape(slot_len, kvs, head_width)
    cosine, sine = rotary_tables(pos_all, head_width)
    cosine, sine = (cosine[:, None, :], sine[:, None, :])

    def turn(q, k, gq, gk):
        return (
            rotate_half(rms_scale(q, gq), cosine, sine),
            rotate_half(rms_scale(k, gk), cosine, sine),
        )

    turned, turn_back = jax.vjp(turn, query_raw, key_raw, gain_query, gain_key)
    query = turned[0].astype(BF).reshape(slot_len, kvs, per, head_width)
    key = turned[1].astype(BF)

    def scores_of():
        raw = jnp.einsum("rkgd,tkd->kgrt", query, key, preferred_element_type=F32) * score_scale
        return jnp.where(allowed, raw, -1e30)

    scores = scores_of()
    row_top = jnp.max(scores, axis=-1, keepdims=True)
    log_total = row_top + jnp.log(jnp.sum(jnp.exp(scores - row_top), axis=-1, keepdims=True))
    probs = jnp.exp(scores - log_total).astype(BF)
    mixed = jnp.einsum("kgrt,tkd->rkgd", probs, value, preferred_element_type=F32)
    mixed = mixed.reshape(slot_len, heads * head_width).astype(BF)
    hidden = inputs + scatter_rows(mm(mixed, output_weight))
    normed2_f, norm_two_back = jax.vjp(rms_scale, hidden, gain_two)
    normed2 = gather_rows(normed2_f.astype(BF))
    active_f, swish_back = jax.vjp(
        lambda a, b: jax.nn.silu(a) * b, mm(normed2, w_gate), mm(normed2, w_up)
    )
    active = active_f.astype(BF)
    output = (valid_rows * (hidden + scatter_rows(mm(active, down_weight)))).astype(BF)
    grad_gate_f, grad_up_f = swish_back(mm_t(grad_branch, down_weight))
    grad_gate, grad_up = (grad_gate_f.astype(BF), grad_up_f.astype(BF))
    grad_hidden_norm, grad_gain_two = norm_two_back(
        scatter_rows(mm_t(grad_gate, w_gate) + mm_t(grad_up, w_up))
    )
    grad_hidden = grad_result + grad_hidden_norm
    grad_mixed_in = gather_rows(grad_hidden.astype(BF))
    grad_mixed = mm_t(grad_mixed_in, output_weight).astype(BF)
    grad_mixed = grad_mixed.reshape(slot_len, kvs, per, head_width)
    probs_f = jnp.exp(scores_of() - log_total)
    grad_probs = jnp.einsum("rkgd,tkd->kgrt", grad_mixed, value, preferred_element_type=F32)
    grad_value = jnp.einsum(
        "kgrt,rkgd->tkd", probs_f.astype(BF), grad_mixed, preferred_element_type=F32
    )
    row_inner = jnp.sum(probs_f * grad_probs, axis=-1, keepdims=True)
    grad_scores = (probs_f * (grad_probs - row_inner)).astype(BF)
    grad_query = (
        jnp.einsum("kgrt,tkd->rkgd", grad_scores, key, preferred_element_type=F32) * score_scale
    )
    grad_key = (
        jnp.einsum("kgrt,rkgd->tkd", grad_scores, query, preferred_element_type=F32) * score_scale
    )
    grad_query_raw, grad_key_raw, grad_gain_query, grad_gain_key = turn_back(
        (grad_query.reshape(slot_len, heads, head_width), grad_key)
    )
    grad_query_b = grad_query_raw.reshape(slot_len, -1).astype(BF)
    grad_key_b = grad_key_raw.reshape(slot_len, -1).astype(BF)
    grad_value_b = grad_value.reshape(slot_len, -1).astype(BF)
    grad_normed = (
        mm_t(grad_query_b, w_qkv[0]) + mm_t(grad_key_b, w_qkv[1]) + mm_t(grad_value_b, w_qkv[2])
    )
    grad_inputs_norm, grad_gain_one = norm_one_back(scatter_rows(grad_normed))
    input_grad = grad_hidden + grad_inputs_norm

    def total(v):
        return lax.psum(v.astype(BF), "replica").astype(F32)

    grad_down = total(mm_w(active, grad_branch))
    grad_gate_w = to_rows(total(mm_w(normed2, grad_gate)).astype(BF)).astype(F32)
    grad_up_w = to_rows(total(mm_w(normed2, grad_up)).astype(BF)).astype(F32)
    grad_output_w = total(mm_w(mixed, grad_mixed_in))
    grad_query_w = to_rows(total(mm_w(normed, grad_query_b)).astype(BF)).astype(F32)
    grad_key_w = to_rows(total(mm_w(normed, grad_key_b)).astype(BF)).astype(F32)
    grad_value_w = to_rows(total(mm_w(normed, grad_value_b)).astype(BF)).astype(F32)
    small = jnp.concatenate([grad_gain_one, grad_gain_two, grad_gain_query, grad_gain_key])
    small = lax.psum(small, ("shard", "replica"))
    at = lax.axis_index("shard")
    hw = query_gain.shape[0]

    def own(start, size):
        return lax.dynamic_slice_in_dim(small, start + at * size, size)

    model = wide * shard_count
    return (
        output[None],
        input_grad[None],
        own(0, wide),
        grad_query_w,
        grad_key_w,
        grad_value_w,
        grad_output_w,
        own(2 * model, hw),
        own(2 * model + head_width, hw),
        own(model, wide),
        grad_gate_w,
        grad_up_w,
        grad_down,
    )


def solution(mesh):
    rows, mat, vec = (P("replica", "shard", None), P("shard", None), P("shard"))
    placed = (rows, rows, P("replica"), P("replica", None), vec, mat, mat, mat, mat)
    placed += (vec, vec, vec, mat, mat, mat)
    outs = (rows, rows, vec, mat, mat, mat, mat, vec, vec, vec, mat, mat, mat)
    return jax.shard_map(shards, mesh=mesh, in_specs=placed, out_specs=outs, check_vma=False)
```

profile of v0, /device:TPU:0, one launch (start us, length us, event | category | flops | bytes accessed | tf_op | source)
XLA Modules:
  0.0 764.7 jit_solution(12287463658765484522)
XLA Ops:
  11.5 8.5 %all-reduce.4 = bf16[2304]{0:T(1024)(128)(2,1)S(1)} all-reduce(bf16[2304]{0:T(1024)(128)(2,1)S(1)} %dynamic-update-slice.3), channel_id=2, replica_groups=mesh['shard'=4,'replica'=8] {'shard'}, use_global_device_ids=true, to_apply=%add.4 | all-reduce | flops 2304 | bytes 9216
  28.5 4.6 compare_select_fusion.1
  33.1 6.2 all-to-all-done.1
  39.3 4.1 all-to-all-start
  47.2 5.5 all-to-all-done
  52.7 4.3 all-to-all-start.2
  64.9 6.6 all-to-all-done.2
  86.3 3.7 exponential_reduce_fusion
  92.0 6.1 convolution_convert_fusion.8
  98.1 3.9 convolution_convert_fusion
  102.1 31.8 %reduce-scatter.5.cloned.1.call-done = bf16[256,1024]{1,0:T(8,128)(2,1)} async-done(((bf16[1024,1024]{1,0:T(8,128)(2,1)}), bf16[256,1024]{1,0:T(8,128)(2,1)}) %reduce-scatter.5.cloned.1.call-update) | async-done | bytes 524304 | tf_op jit(solution)/shard_map/reduce_scatter | solution.py:50
  139.8 4.3 all-to-all-start.3
  149.6 25.8 %all-to-all-done.3 = bf16[256,4,768]{0,2,1:T(8,128)(2,1)} async-done(((bf16[256,4,768]{0,2,1:T(8,128)(2,1)}), bf16[256,4,768]{0,2,1:T(8,128)(2,1)}, u32[]{:S(2)}, u32[]{:S(2)}) %all-to-all-start.3) | async-done | bytes 1572896 | tf_op jit(solution)/shard_map/all_to_all | solution.py:54
  175.4 4.4 all-to-all-start.4
  182.7 28.1 %all-to-all-done.4 = bf16[256,4,768]{0,2,1:T(8,128)(2,1)} async-done(((bf16[256,4,768]{0,2,1:T(8,128)(2,1)}), bf16[256,4,768]{0,2,1:T(8,128)(2,1)}, u32[]{:S(2)}, u32[]{:S(2)}) %all-to-all-start.4) | async-done | bytes 1572896 | tf_op jit(solution)/shard_map/all_to_all | solution.py:54
  213.4 5.6 fusion.63
  222.5 7.2 multiply_convert_fusion
  235.5 31.5 %reduce-scatter.9.cloned.1.call-done = bf16[256,1024]{1,0:T(8,128)(2,1)} async-done(((bf16[1024,1024]{1,0:T(8,128)(2,1)}), bf16[256,1024]{1,0:T(8,128)(2,1)}) %reduce-scatter.9.cloned.1.call-update) | async-done | bytes 524304 | tf_op jit(solution)/shard_map/reduce_scatter | solution.py:50
  271.8 5.2 convolution_convert_fusion.3
  283.1 11.0 %all-gather.12.cloned.1.call-done = bf16[1024,1024]{1,0:T(8,128)(2,1)} async-done(((bf16[256,1024]{1,0:T(8,128)(2,1)}), bf16[1024,1024]{1,0:T(8,128)(2,1)}) %all-gather.12.cloned.1.call-update) | async-done | bytes 2097168 | tf_op jit(solution)/shard_map/all_gather | solution.py:46
  297.2 8.5 %fusion.18 = bf16[2,128,1024]{2,1,0:T(8,128)(2,1)S(1)} fusion(bf16[1024,2,2,128]{0,3,2,1:T(8,128)(2,1)S(1)} %bitcast.261, f32[2,1024,1024,2]{2,1,3,0:T(8,128)} %copy-done.1, f32[2,2,1024]{2,1,0:T(2,128)S(1)} %log_add_fusion, pred[1024,1024]{0,1:T(8,128)(4,1)S(1)} %broadcast_compare_fusion), kind=kOutput, calls=%fused_computation.65 | convolution fusion | flops 1090781184 | bytes 19415040 | tf_op jit(solution)/shard_map/kgrt,rkgd->tkd/dot_general | solution.py:156
  305.8 12.4 %fusion = (f32[2,2,1024]{2,1,0:T(2,128)S(1)}, f32[2,1024,1024,2]{2,1,3,0:T(8,128)}) fusion(f32[2,1024,1024,2]{2,1,3,0:T(8,128)} %copy-done.1, f32[2,2,1024]{2,1,0:T(2,128)S(1)} %log_add_fusion, pred[1024,1024]{0,1:T(8,128)(4,1)S(1)} %broadcast_compare_fusion, bf16[1024,2,128,1]{0,2,3,1:T(8,128)(2,1)S(1)} %bitcast.264, bf16[1024,2,2,128]{0,3,2,1:T(8,128)(2,1)S(1)} %bitcast.262), kind=kOutput, calls=%fused_computation.2 | convolution fusion | flops 1094709248 | bytes 36208640 | tf_op jit(solution)/shard_map/rkgd,tkd->kgrt/dot_general | solution.py:155
  318.2 12.4 %fusion.2 = bf16[2,2,1024,1024]{2,3,1,0:T(8,128)(2,1)S(1)} fusion(f32[2,1024,1024,2]{2,1,3,0:T(8,128)} %get-tuple-element.84, f32[2,1024,1024,2]{2,1,3,0:T(8,128)} %copy-done.1, f32[2,2,1024]{2,1,0:T(2,128)S(1)} %get-tuple-element.83, f32[2,2,1024]{2,1,0:T(2,128)S(1)} %log_add_fusion, pred[1024,1024]{0,1:T(8,128)(4,1)S(1)} %broadcast_compare_fusion), kind=kLoop, calls=%fused_computation.4 | loop fusion | flops 25165824 | bytes 43024384 | tf_op jit(solution)/shard_map/convert_element_type | solution.py:160
  354.6 3.9 add_convert_fusion
  358.5 4.5 convolution_convert_fusion.1
  363.1 247.1 %all-reduce.8.cloned.1.call-done = (bf16[4,256,512]{2,1,0:T(8,128)(2,1)}, bf16[4,256,256]{2,1,0:T(8,128)(2,1)}, bf16[4,256,256]{2,1,0:T(8,128)(2,1)}, bf16[512,1...) async-done(((bf16[4,256,512]{2,1,0:T(8,128)(2,1)}, bf16[4,256,256]{2,1,0:T(8,128)(2,1)}, ...) | async-done | bytes 7864336 | tf_op jit(solution)/shard_map/psum | solution.py:180
  610.2 13.2 %all_to_all.160 = bf16[4,256,256]{2,1,0:T(8,128)(2,1)} all-to-all(bf16[4,256,256]{2,1,0:T(8,128)(2,1)} %get-tuple-element.34), channel_id=1, replica_groups=mesh['shard'=4,'replica'=8] {'shard'}, dimensions={0} | all-to-all | bytes 1048576 | tf_op jit(solution)/shard_map/all_to_all | solution.py:58
  623.4 18.6 %all_to_all.161 = bf16[4,256,256]{2,1,0:T(8,128)(2,1)} all-to-all(bf16[4,256,256]{2,1,0:T(8,128)(2,1)} %get-tuple-element.35), channel_id=1, replica_groups=mesh['shard'=4,'replica'=8] {'shard'}, dimensions={0} | all-to-all | bytes 1048576 | tf_op jit(solution)/shard_map/all_to_all | solution.py:58
  642.0 17.6 %all_to_all.162 = bf16[4,256,512]{2,1,0:T(8,128)(2,1)} all-to-all(bf16[4,256,512]{2,1,0:T(8,128)(2,1)S(1)} %copy-done.34), channel_id=1, replica_groups=mesh['shard'=4,'replica'=8] {'shard'}, dimensions={0} | all-to-all | bytes 2097152 | tf_op jit(solution)/shard_map/all_to_all | solution.py:58
  659.6 4.5 all-to-all-start.9
  665.7 62.1 %psum.56 = f32[2304]{0:T(1024)S(1)} all-reduce(f32[2304]{0:T(1024)S(1)} %pad_maximum_fusion.1), channel_id=1, replica_groups=mesh['shard'=4,'replica'=8] {'shard','replica'}, use_global_device_ids=true, to_apply=%region_19.20 | all-reduce | flops 2304 | bytes 18432 | tf_op jit(solution)/shard_map/psum | solution.py:190
  749.1 6.4 all-to-all-done.8
  (231 shorter events, 128.6 us)
Async XLA Ops:
  7.2 215.3 %copy-start = (bf16[768,1024]{1,0:T(8,128)(2,1)S(1)}, bf16[768,1024]{1,0:T(8,128)(2,1)}, u32[]{:S(2)}) copy-start(bf16[768,1024]{1,0:T(8,128)(2,1)} %param.31) | copy-start | bytes 4718596
  7.2 15.0 %copy-start.39 = (bf16[256,1024]{1,0:T(8,128)(2,1)S(1)}, bf16[256,1024]{1,0:T(8,128)(2,1)}, u32[]{:S(2)}) copy-start(bf16[256,1024]{1,0:T(8,128)(2,1)} %param.23) | copy-start | bytes 1572868
  7.2 66.6 %all-gather.6.cloned.1.call-start = ((), (), s32[]{:S(2)}) async-start(), calls=%async_computation.14 | async-start | bytes 2621440 | tf_op jit(solution)/shard_map/all_gather | solution.py:46
  23.4 15.9 %all-to-all-start.1 = ((bf16[256,4,256]{2,0,1:T(8,128)(2,1)}), bf16[256,4,256]{2,0,1:T(8,128)(2,1)S(1)}, u32[]{:S(2)}, u32[]{:S(2)}) async-start(bf16[256,4,256]{2,0,1:T(8,128)(2,1)} %copy.103), calls=%async_computation.1 | async-start | bytes 1048576 | tf_op jit(solution)/shard_map/all_to_all | solution.py:54
  39.3 7.2 copy-start.13
  39.3 13.4 %all-to-all-start = ((bf16[256,4,256]{0,2,1:T(8,128)(2,1)}), bf16[256,4,256]{0,2,1:T(8,128)(2,1)}, u32[]{:S(2)}, u32[]{:S(2)}) async-start(bf16[256,4,256]{0,2,1:T(8,128)(2,1)} %bitcast.17), calls=%async_computation | async-start | bytes 1048576 | tf_op jit(solution)/shard_map/all_to_all | solution.py:54
  52.7 18.8 %all-to-all-start.2 = ((bf16[256,4,512]{2,0,1:T(8,128)(2,1)}), bf16[256,4,512]{2,0,1:T(8,128)(2,1)}, u32[]{:S(2)}, u32[]{:S(2)}) async-start(bf16[256,4,512]{2,0,1:T(8,128)(2,1)} %copy.106), calls=%async_computation.2 | async-start | bytes 2097152 | tf_op jit(solution)/shard_map/all_to_all | solution.py:54
  57.0 76.9 %reduce-scatter.5.cloned.1.call-start = ((), (), s32[]{:S(2)}) async-start(), calls=%async_computation.15 | async-start | bytes 2621440 | tf_op jit(solution)/shard_map/reduce_scatter | solution.py:50
  60.2 21.9 %copy-start.8 = (f32[1024,128]{0,1:T(8,128)}, f32[1024,128]{0,1:T(8,128)S(1)}, u32[]{:S(2)}) copy-start(f32[1024,128]{0,1:T(8,128)S(1)} %get-tuple-element.60) | copy-start | bytes 1572868
  86.3 5.8 copy-start.1
  90.8 7.3 copy-start.36
  92.0 6.1 copy-start.48
  102.0 31.9 %copy-start.4 = (bf16[1,256,1024]{2,1,0:T(8,128)(2,1)S(1)}, bf16[1,256,1024]{2,1,0:T(8,128)(2,1)}, u32[]{:S(2)}) copy-start(bf16[1,256,1024]{2,1,0:T(8,128)(2,1)} %param.17) | copy-start | bytes 1572868
  102.0 111.4 %all-gather.8.cloned.1.call-start = ((), (), s32[]{:S(2)}) async-start(), calls=%async_computation.16 | async-start | bytes 2621440 | tf_op jit(solution)/shard_map/all_gather | solution.py:46
  139.8 35.6 %all-to-all-start.3 = ((bf16[256,4,768]{0,2,1:T(8,128)(2,1)}), bf16[256,4,768]{0,2,1:T(8,128)(2,1)}, u32[]{:S(2)}, u32[]{:S(2)}) async-start(bf16[256,4,768]{0,2,1:T(8,128)(2,1)} %bitcast.234), calls=%async_computation.4 | async-start | bytes 3145728 | tf_op jit(solution)/shard_map/all_to_all | solution.py:54
  144.2 78.3 %all-gather.10.cloned.1.call-start = ((), (), s32[]{:S(2)}) async-start(), calls=%async_computation.18 | async-start | bytes 2621440 | tf_op jit(solution)/shard_map/all_gather | solution.py:46
  175.4 35.4 %all-to-all-start.4 = ((bf16[256,4,768]{0,2,1:T(8,128)(2,1)}), bf16[256,4,768]{0,2,1:T(8,128)(2,1)}, u32[]{:S(2)}, u32[]{:S(2)}) async-start(bf16[256,4,768]{0,2,1:T(8,128)(2,1)} %bitcast.235), calls=%async_computation.5 | async-start | bytes 3145728 | tf_op jit(solution)/shard_map/all_to_all | solution.py:54
  179.8 87.2 %reduce-scatter.9.cloned.1.call-start = ((), (), s32[]{:S(2)}) async-start(), calls=%async_computation.19 | async-start | bytes 2621440 | tf_op jit(solution)/shard_map/reduce_scatter | solution.py:50
  222.5 7.2 copy-start.31
  235.4 58.6 %all-gather.12.cloned.1.call-start = ((), (), s32[]{:S(2)}) async-start(), calls=%async_computation.20 | async-start | bytes 2621440 | tf_op jit(solution)/shard_map/all_gather | solution.py:46
  271.3 338.9 %all-reduce.8.cloned.1.call-start = ((), (), s32[]{:S(2)}) async-start(), calls=%async_computation.22 | async-start | bytes 15728640 | tf_op jit(solution)/shard_map/psum | solution.py:180
  297.2 8.5 %copy-start.37 = (bf16[1024,256]{0,1:T(8,128)(2,1)S(1)}, bf16[1024,256]{0,1:T(8,128)(2,1)}, u32[]{:S(2)}) copy-start(bf16[1024,256]{0,1:T(8,128)(2,1)} %copy-done.36) | copy-start | bytes 1572868
  305.8 39.2 %copy-start.38 = (bf16[2,128,1024]{2,1,0:T(8,128)(2,1)}, bf16[2,128,1024]{2,1,0:T(8,128)(2,1)S(1)}, u32[]{:S(2)}) copy-start(bf16[2,128,1024]{2,1,0:T(8,128)(2,1)S(1)} %fusion.18) | copy-start | bytes 1572868
  318.2 12.4 %copy-start.29 = (bf16[1024,2,128,1]{0,2,3,1:T(8,128)(2,1)S(1)}, bf16[1024,2,128,1]{0,2,3,1:T(8,128)(2,1)}, u32[]{:S(2)}) copy-start(bf16[1024,2,128,1]{0,2,3,1:T(8,128)(2,1)} %copy-done.28) | copy-start | bytes 1572868
  340.6 5.9 copy-start.25
  350.4 313.7 %reduce-scatter.11.cloned.1.call-start = ((), (), s32[]{:S(2)}) async-start(), calls=%async_computation.21 | async-start | bytes 2621440 | tf_op jit(solution)/shard_map/reduce_scatter | solution.py:50
  358.5 370.0 %reduce-scatter.7.cloned.1.call-start = ((), (), s32[]{:S(2)}) async-start(), calls=%async_computation.17 | async-start | bytes 2621440 | tf_op jit(solution)/shard_map/reduce_scatter | solution.py:50
  610.2 31.7 %copy-start.34 = (bf16[4,256,512]{2,1,0:T(8,128)(2,1)S(1)}, bf16[4,256,512]{2,1,0:T(8,128)(2,1)}, u32[]{:S(2)}) copy-start(bf16[4,256,512]{2,1,0:T(8,128)(2,1)} %get-tuple-element.33) | copy-start | bytes 3145732
  659.6 68.9 %copy-start.7 = (bf16[256,1024]{1,0:T(8,128)(2,1)S(1)}, bf16[256,1024]{1,0:T(8,128)(2,1)}, u32[]{:S(2)}) copy-start(bf16[256,1024]{1,0:T(8,128)(2,1)} %reduce-scatter.5.cloned.1.call-done) | copy-start | bytes 1572868
  659.6 68.9 %copy-start.12 = (bf16[1,256,1024]{2,1,0:T(8,128)(2,1)S(1)}, bf16[1,256,1024]{2,1,0:T(8,128)(2,1)}, u32[]{:S(2)}) copy-start(bf16[1,256,1024]{2,1,0:T(8,128)(2,1)} %param.18) | copy-start | bytes 1572868
  659.6 72.2 %all-to-all-start.9 = ((bf16[4,256,768]{2,1,0:T(8,128)(2,1)}), bf16[4,256,768]{2,1,0:T(8,128)(2,1)}, u32[]{:S(2)}, u32[]{:S(2)}) async-start(bf16[4,256,768]{2,1,0:T(8,128)(2,1)} %get-tuple-element.38), calls=%async_computation.13 | async-start | bytes 3145728 | tf_op jit(solution)/shard_map/all_to_all | solution.py:58
  731.9 23.7 %all-to-all-start.8 = ((bf16[4,256,768]{2,1,0:T(8,128)(2,1)}), bf16[4,256,768]{2,1,0:T(8,128)(2,1)S(1)}, u32[]{:S(2)}, u32[]{:S(2)}) async-start(bf16[4,256,768]{2,1,0:T(8,128)(2,1)} %get-tuple-element.37), calls=%async_computation.12 | async-start | bytes 3145728 | tf_op jit(solution)/shard_map/all_to_all | solution.py:58
  (38 other events, 100.4 us)
Sparse Core Ops, SparseCore 0:
  22.3 26.2 all-gather.5
  102.1 31.7 reduce-scatter.4
  137.4 33.7 all-gather.7
  172.7 33.7 all-gather.9
  235.6 31.4 reduce-scatter.8
  271.5 22.5 all-gather.11
  350.6 259.6 all-reduce.7
  613.3 35.3 reduce-scatter.10
  652.0 42.2 reduce-scatter.6
where the time goes:
time: 769 us; the launch traced here: 765 us
  waiting for transfers between devices  400 us (52%)
  blocking collectives  120 us (16%)
  matrix products  97.4 us (13%)
  other arithmetic  56.2 us (7%)
  local copies, waits for them, and re-layouts  44.7 us (6%)
  starting transfers between devices  29.9 us (4%)
  between operations  16.3 us (2%)
    psum x1, waiting for transfers between devices, total(): return lax.psum(v.astype(BF), 'replica').astype(F32)  247 us
    all_to_all x5, waiting for transfers between devices, to_columns(): return lax.all_to_all(w, 'shard', split_axis=1, concat_axis=0, tiled=True)  72.1 us
    reduce_scatter x4, waiting for transfers between devices, scatter_rows(): lax.psum_scatter(v.astype(BF), 'shard', scatter_dimension=0, tiled=True)  63.4 us
    psum x1, blocking collectives, shards(): small = lax.psum(small, ('shard', 'replica'))  62.1 us
    all_to_all x3, blocking collectives, to_rows(): return lax.all_to_all(g, 'shard', split_axis=0, concat_axis=1, tiled=True)  49.4 us
    dot_general x7, matrix products, mm(): return jnp.einsum('ri,io->ro', a, b, preferred_element_type=F32)  22 us
    dot_general x7, matrix products, mm_t(): return jnp.einsum('ro,io->ri', a, b, preferred_element_type=F32)  21.9 us
    all_to_all x5, starting transfers between devices, to_columns(): return lax.all_to_all(w, 'shard', split_axis=1, concat_axis=0, tiled=True)  20.6 us
  transfers between devices with their start and end apart: 16, of which 10 were waited for; matrix products, arithmetic and copies ran while one was open for 11% of the time, Pallas kernels for 0%

commit v1 on v0

--- a/solution.py
+++ b/solution.py
@@ -177,7 +177,7 @@
     input_grad = grad_hidden + grad_inputs_norm
 
     def total(v):
-        return lax.psum(v.astype(BF), "replica").astype(F32)
+        return jnp.sum(lax.all_gather(v.astype(BF), "replica"), axis=0).astype(F32)
 
     grad_down = total(mm_w(active, grad_branch))
     grad_gate_w = to_rows(total(mm_w(normed2, grad_gate)).astype(BF)).astype(F32)

time: 769 us -> 1400 us (1.82)
  waiting for transfers between devices: 400 us -> 999 us
  blocking collectives: 120 us -> 48 us
  other arithmetic: 56.2 us -> 107 us
  local copies, waits for them, and re-layouts: 44.7 us -> 66.5 us
  matrix products: 97.4 us -> 119 us
    all_gather x0 -> x7, waiting for transfers between devices: none -> 810 us  [total(): return jnp.sum(lax.all_gather(v.astype(BF), 'replica'), axis=0).astype(F32)]
    psum x1 -> x0, waiting for transfers between devices: 247 us -> none  [total(): return lax.psum(v.astype(BF), 'replica').astype(F32)]
    all_to_all x3 -> x0, blocking collectives: 49.4 us -> none  [to_rows(): return lax.all_to_all(g, 'shard', split_axis=0, concat_axis=1, tiled=True)]
    reduce_sum x0 -> x7, other arithmetic: none -> 44.1 us  [total(): return jnp.sum(lax.all_gather(v.astype(BF), 'replica'), axis=0).astype(F32)]
    reduce_scatter x4, waiting for transfers between devices: 63.4 us -> 94.1 us  [scatter_rows(): lax.psum_scatter(v.astype(BF), 'shard', scatter_dimension=0, tiled=True)]
    psum x1, blocking collectives: 62.1 us -> 39.5 us  [shards(): small = lax.psum(small, ('shard', 'replica'))]
    unnamed x118 -> x135, local copies, waits for them, and re-layouts: 20.5 us -> 38 us
  transfers between devices with their start and end apart: 16 -> 25, of which waited for: 10 -> 16; matrix products, arithmetic and copies ran while one was open for 11% -> 13% of each run, Pallas kernels for 0% -> 0%
where the time goes in v1:
time: 1400 us
  waiting for transfers between devices  999 us (71%)
  matrix products  119 us (8%)
  other arithmetic  107 us (8%)
  local copies, waits for them, and re-layouts  66.5 us (5%)
  blocking collectives  48 us (3%)
  starting transfers between devices  42.1 us (3%)
  between operations  16.4 us (1%)
    all_gather x7, waiting for transfers between devices, total(): return jnp.sum(lax.all_gather(v.astype(BF), 'replica'), axis=0).astype(F32)  810 us
    reduce_scatter x4, waiting for transfers between devices, scatter_rows(): lax.psum_scatter(v.astype(BF), 'shard', scatter_dimension=0, tiled=True)  94.1 us
    all_to_all x5, waiting for transfers between devices, to_columns(): return lax.all_to_all(w, 'shard', split_axis=1, concat_axis=0, tiled=True)  72.6 us
    reduce_sum x7, other arithmetic, total(): return jnp.sum(lax.all_gather(v.astype(BF), 'replica'), axis=0).astype(F32)  44.1 us
    psum x1, blocking collectives, shards(): small = lax.psum(small, ('shard', 'replica'))  39.5 us
    unnamed x135, local copies, waits for them, and re-layouts  38 us
  transfers between devices with their start and end apart: 25, of which 16 were waited for; matrix products, arithmetic and copies ran while one was open for 13% of the time, Pallas kernels for 0%

profile of v1, /device:TPU:0, one launch (start us, length us, event | category | flops | bytes accessed | tf_op | source)
XLA Modules:
  0.0 1398.4 jit_solution(9857178563039373314)
XLA Ops:
  10.3 8.5 all-reduce.4
  33.1 6.2 all-to-all-done.1
  47.2 5.5 all-to-all-done
  65.1 6.4 all-to-all-done.2
  92.1 15.9 %convolution_convert_fusion.8 = bf16[2,128,2,1024]{3,1,2,0:T(8,128)(2,1)} fusion(bf16[1024,2,128,1]{0,2,3,1:T(8,128)(2,1)S(1)} %bitcast.273, f32[2,1024,1024,2]{2,1,3,0:T(8,128)S(1)} %get-tuple-element.114, f32[2,2,1024]{2,1,0:T(2,128)S(1)} %log_add_fusion, pred[1024,1024]{0,1:T(8,128)(4,1)S(1)} %broadcast_compare_fusion), kind=kOutput, calls=%fused_computation.58 | convolution fusion | flops 1091043328 | bytes 19415040 | tf_op jit(solution)/shard_map/kgrt,tkd->rkgd/dot_general | solution.py:135
  112.0 31.8 %reduce-scatter.5.cloned.1.call-done = bf16[256,1024]{1,0:T(8,128)(2,1)} async-done(((bf16[1024,1024]{1,0:T(8,128)(2,1)}), bf16[256,1024]{1,0:T(8,128)(2,1)}) %reduce-scatter.5.cloned.1.call-update) | async-done | bytes 524304 | tf_op jit(solution)/shard_map/reduce_scatter | solution.py:50
  159.5 25.8 %all-to-all-done.3 = bf16[256,4,768]{0,2,1:T(8,128)(2,1)} async-done(((bf16[256,4,768]{0,2,1:T(8,128)(2,1)}), bf16[256,4,768]{0,2,1:T(8,128)(2,1)}, u32[]{:S(2)}, u32[]{:S(2)}) %all-to-all-start.3) | async-done | bytes 1572896 | tf_op jit(solution)/shard_map/all_to_all | solution.py:54
  192.4 28.7 %all-to-all-done.4 = bf16[256,4,768]{0,2,1:T(8,128)(2,1)} async-done(((bf16[256,4,768]{0,2,1:T(8,128)(2,1)}), bf16[256,4,768]{0,2,1:T(8,128)(2,1)}, u32[]{:S(2)}, u32[]{:S(2)}) %all-to-all-start.4) | async-done | bytes 1572896 | tf_op jit(solution)/shard_map/all_to_all | solution.py:54
  223.6 5.6 fusion.62
  232.8 7.3 multiply_convert_fusion
  245.8 31.5 %reduce-scatter.9.cloned.1.call-done = bf16[256,1024]{1,0:T(8,128)(2,1)} async-done(((bf16[1024,1024]{1,0:T(8,128)(2,1)}), bf16[256,1024]{1,0:T(8,128)(2,1)}) %reduce-scatter.9.cloned.1.call-update) | async-done | bytes 524304 | tf_op jit(solution)/shard_map/reduce_scatter | solution.py:50
  281.7 22.7 %all-gather.26.cloned.1.call-done = bf16[1024,1024]{1,0:T(8,128)(2,1)} async-done(((bf16[256,1024]{1,0:T(8,128)(2,1)}), bf16[1024,1024]{1,0:T(8,128)(2,1)}) %all-gather.26.cloned.1.call-update) | async-done | bytes 2097168 | tf_op jit(solution)/shard_map/all_gather | solution.py:46
  307.6 12.7 fusion
  320.4 12.6 fusion.2
  341.9 10.9 fusion.18
  367.0 5.1 convolution_convert_fusion.4
  384.2 5.2 convolution_convert_fusion.3
  393.4 5.1 convolution_convert_fusion.2
  398.5 16.5 %all-gather.30.cloned.1.call-done = bf16[8192,256]{1,0:T(8,128)(2,1)} async-done(((bf16[1024,256]{1,0:T(8,128)(2,1)}), bf16[8192,256]{1,0:T(8,128)(2,1)}) %all-gather.30.cloned.1.call-update) | async-done | bytes 4194320 | tf_op jit(solution)/shard_map/all_gather | solution.py:180
  422.2 66.6 %all-gather.32.cloned.1.call-done = bf16[8192,256]{1,0:T(8,128)(2,1)} async-done(((bf16[1024,256]{1,0:T(8,128)(2,1)}), bf16[8192,256]{1,0:T(8,128)(2,1)}) %all-gather.32.cloned.1.call-update) | async-done | bytes 4194320 | tf_op jit(solution)/shard_map/all_gather | solution.py:180
  496.0 118.7 %all-gather.28.cloned.1.call-done = bf16[8192,512]{1,0:T(8,128)(2,1)} async-done(((bf16[1024,512]{1,0:T(8,128)(2,1)}), bf16[8192,512]{1,0:T(8,128)(2,1)}) %all-gather.28.cloned.1.call-update) | async-done | bytes 8388624 | tf_op jit(solution)/shard_map/all_gather | solution.py:180
  614.7 5.9 reduce_sum.256
  625.2 166.8 %all-gather.36.cloned.1.call-done = bf16[8192,768]{1,0:T(8,128)(2,1)} async-done(((bf16[1024,768]{1,0:T(8,128)(2,1)}), bf16[8192,768]{1,0:T(8,128)(2,1)}) %all-gather.36.cloned.1.call-update) | async-done | bytes 12582928 | tf_op jit(solution)/shard_map/all_gather | solution.py:180
  792.0 7.9 reduce_sum.260
  805.4 30.7 %reduce-scatter.11.cloned.1.call-done = bf16[256,1024]{1,0:T(8,128)(2,1)} async-done(((bf16[1024,1024]{1,0:T(8,128)(2,1)}), bf16[256,1024]{1,0:T(8,128)(2,1)}) %reduce-scatter.11.cloned.1.call-update) | async-done | bytes 524304 | tf_op jit(solution)/shard_map/reduce_scatter | solution.py:50
  837.6 39.5 %psum.7 = f32[2304]{0:T(1024)S(1)} all-reduce(f32[2304]{0:T(1024)S(1)} %pad_maximum_fusion.1), channel_id=1, replica_groups=mesh['shard'=4,'replica'=8] {'shard','replica'}, use_global_device_ids=true, to_apply=%region_19.20 | all-reduce | flops 2304 | bytes 18432 | tf_op jit(solution)/shard_map/psum | solution.py:190
  881.2 167.6 %all-gather.38.cloned.1.call-done = bf16[8192,768]{1,0:T(8,128)(2,1)} async-done(((bf16[1024,768]{1,0:T(8,128)(2,1)}), bf16[8192,768]{1,0:T(8,128)(2,1)}) %all-gather.38.cloned.1.call-update) | async-done | bytes 12582928 | tf_op jit(solution)/shard_map/all_gather | solution.py:180
  1048.8 7.9 reduce_sum.261
  1070.0 103.9 %all-gather.34.cloned.1.call-done = bf16[4096,1024]{1,0:T(8,128)(2,1)} async-done(((bf16[512,1024]{1,0:T(8,128)(2,1)}), bf16[4096,1024]{1,0:T(8,128)(2,1)}) %all-gather.34.cloned.1.call-update) | async-done | bytes 8388624 | tf_op jit(solution)/shard_map/all_gather | solution.py:180
  1173.9 5.7 reduce_sum.259
  1181.1 169.5 %all-gather.40.cloned.1.call-done = bf16[6144,1024]{1,0:T(8,128)(2,1)} async-done(((bf16[768,1024]{1,0:T(8,128)(2,1)}), bf16[6144,1024]{1,0:T(8,128)(2,1)}) %all-gather.40.cloned.1.call-update) | async-done | bytes 12582928 | tf_op jit(solution)/shard_map/all_gather | solution.py:180
  1350.6 9.3 reduce_sum.262
  (276 shorter events, 217.9 us)
Async XLA Ops:
  7.2 225.6 %copy-start = (bf16[768,1024]{1,0:T(8,128)(2,1)S(1)}, bf16[768,1024]{1,0:T(8,128)(2,1)}, u32[]{:S(2)}) copy-start(bf16[768,1024]{1,0:T(8,128)(2,1)} %param.31) | copy-start | bytes 4718596
  7.2 66.6 %all-gather.20.cloned.1.call-start = ((), (), s32[]{:S(2)}) async-start(), calls=%async_computation.14 | async-start | bytes 2621440 | tf_op jit(solution)/shard_map/all_gather | solution.py:46
  23.5 15.9 %all-to-all-start.1 = ((bf16[256,4,256]{2,0,1:T(8,128)(2,1)}), bf16[256,4,256]{2,0,1:T(8,128)(2,1)S(1)}, u32[]{:S(2)}, u32[]{:S(2)}) async-start(bf16[256,4,256]{2,0,1:T(8,128)(2,1)} %copy.103), calls=%async_computation.1 | async-start | bytes 1048576 | tf_op jit(solution)/shard_map/all_to_all | solution.py:54
  39.3 13.4 all-to-all-start
  52.7 18.8 %all-to-all-start.2 = ((bf16[256,4,512]{2,0,1:T(8,128)(2,1)}), bf16[256,4,512]{2,0,1:T(8,128)(2,1)}, u32[]{:S(2)}, u32[]{:S(2)}) async-start(bf16[256,4,512]{2,0,1:T(8,128)(2,1)} %copy.106), calls=%async_computation.2 | async-start | bytes 2097152 | tf_op jit(solution)/shard_map/all_to_all | solution.py:54
  57.0 86.8 %reduce-scatter.5.cloned.1.call-start = ((), (), s32[]{:S(2)}) async-start(), calls=%async_computation.15 | async-start | bytes 2621440 | tf_op jit(solution)/shard_map/reduce_scatter | solution.py:50
  111.9 111.7 %all-gather.22.cloned.1.call-start = ((), (), s32[]{:S(2)}) async-start(), calls=%async_computation.16 | async-start | bytes 2621440 | tf_op jit(solution)/shard_map/all_gather | solution.py:46
  149.7 35.6 %all-to-all-start.3 = ((bf16[256,4,768]{0,2,1:T(8,128)(2,1)}), bf16[256,4,768]{0,2,1:T(8,128)(2,1)}, u32[]{:S(2)}, u32[]{:S(2)}) async-start(bf16[256,4,768]{0,2,1:T(8,128)(2,1)} %bitcast.244), calls=%async_computation.4 | async-start | bytes 3145728 | tf_op jit(solution)/shard_map/all_to_all | solution.py:54
  154.1 78.7 %all-gather.24.cloned.1.call-start = ((), (), s32[]{:S(2)}) async-start(), calls=%async_computation.18 | async-start | bytes 2621440 | tf_op jit(solution)/shard_map/all_gather | solution.py:46
  185.3 35.7 %all-to-all-start.4 = ((bf16[256,4,768]{0,2,1:T(8,128)(2,1)}), bf16[256,4,768]{0,2,1:T(8,128)(2,1)}, u32[]{:S(2)}, u32[]{:S(2)}) async-start(bf16[256,4,768]{0,2,1:T(8,128)(2,1)} %bitcast.245), calls=%async_computation.5 | async-start | bytes 3145728 | tf_op jit(solution)/shard_map/all_to_all | solution.py:54
  189.7 87.7 %reduce-scatter.9.cloned.1.call-start = ((), (), s32[]{:S(2)}) async-start(), calls=%async_computation.19 | async-start | bytes 2621440 | tf_op jit(solution)/shard_map/reduce_scatter | solution.py:50
  245.7 58.6 %all-gather.26.cloned.1.call-start = ((), (), s32[]{:S(2)}) async-start(), calls=%async_computation.20 | async-start | bytes 2621440 | tf_op jit(solution)/shard_map/all_gather | solution.py:46
  281.6 133.3 %all-gather.30.cloned.1.call-start = ((), (), s32[]{:S(2)}) async-start(), calls=%async_computation.23 | async-start | bytes 4718592 | tf_op jit(solution)/shard_map/all_gather | solution.py:180
  341.4 147.4 %all-gather.32.cloned.1.call-start = ((), (), s32[]{:S(2)}) async-start(), calls=%async_computation.24 | async-start | bytes 4718592 | tf_op jit(solution)/shard_map/all_gather | solution.py:180
  355.2 259.5 %all-gather.28.cloned.1.call-start = ((), (), s32[]{:S(2)}) async-start(), calls=%async_computation.22 | async-start | bytes 9437184 | tf_op jit(solution)/shard_map/all_gather | solution.py:180
  366.9 425.1 %all-gather.36.cloned.1.call-start = ((), (), s32[]{:S(2)}) async-start(), calls=%async_computation.26 | async-start | bytes 14155776 | tf_op jit(solution)/shard_map/all_gather | solution.py:180
  372.1 464.0 %reduce-scatter.11.cloned.1.call-start = ((), (), s32[]{:S(2)}) async-start(), calls=%async_computation.21 | async-start | bytes 2621440 | tf_op jit(solution)/shard_map/reduce_scatter | solution.py:50
  379.5 498.2 %reduce-scatter.7.cloned.1.call-start = ((), (), s32[]{:S(2)}) async-start(), calls=%async_computation.17 | async-start | bytes 2621440 | tf_op jit(solution)/shard_map/reduce_scatter | solution.py:50
  384.2 664.6 %all-gather.38.cloned.1.call-start = ((), (), s32[]{:S(2)}) async-start(), calls=%async_computation.27 | async-start | bytes 14155776 | tf_op jit(solution)/shard_map/all_gather | solution.py:180
  389.4 784.5 %all-gather.34.cloned.1.call-start = ((), (), s32[]{:S(2)}) async-start(), calls=%async_computation.25 | async-start | bytes 9437184 | tf_op jit(solution)/shard_map/all_gather | solution.py:180
  393.3 957.3 %all-gather.40.cloned.1.call-start = ((), (), s32[]{:S(2)}) async-start(), calls=%async_computation.28 | async-start | bytes 14155776 | tf_op jit(solution)/shard_map/all_gather | solution.py:180
  418.7 73.8 %all-to-all-start.6 = ((bf16[4,256,256]{2,1,0:T(8,128)(2,1)}), bf16[4,256,256]{2,1,0:T(8,128)(2,1)S(1)}, u32[]{:S(2)}, u32[]{:S(2)}) async-start(bf16[4,256,256]{2,1,0:T(8,128)(2,1)} %bitcast.73), calls=%async_computation.10 | async-start | bytes 1048576 | tf_op jit(solution)/shard_map/all_to_all | solution.py:58
  492.5 128.1 %copy-start.25 = (bf16[4,256,256]{2,1,0:T(8,128)(2,1)}, bf16[4,256,256]{2,1,0:T(8,128)(2,1)S(1)}, u32[]{:S(2)}) copy-start(bf16[4,256,256]{2,1,0:T(8,128)(2,1)S(1)} %all-to-all-done.6) | copy-start | bytes 1572868
  492.5 128.1 %all-to-all-start.7 = ((bf16[4,256,256]{2,1,0:T(8,128)(2,1)}), bf16[4,256,256]{2,1,0:T(8,128)(2,1)S(1)}, u32[]{:S(2)}, u32[]{:S(2)}) async-start(bf16[4,256,256]{2,1,0:T(8,128)(2,1)} %bitcast.262), calls=%async_computation.11 | async-start | bytes 1048576 | tf_op jit(solution)/shard_map/all_to_all | solution.py:58
  621.4 178.5 %all-to-all-start.5 = ((bf16[4,256,512]{2,1,0:T(8,128)(2,1)}), bf16[4,256,512]{2,1,0:T(8,128)(2,1)S(1)}, u32[]{:S(2)}, u32[]{:S(2)}) async-start(bf16[4,256,512]{2,1,0:T(8,128)(2,1)} %bitcast.252), calls=%async_computation.9 | async-start | bytes 2097152 | tf_op jit(solution)/shard_map/all_to_all | solution.py:58
  799.9 36.2 %copy-start.45 = (f32[1,2,4,128]{3,1,2,0:T(2,128)S(1)}, f32[1,2,4,128]{3,1,2,0:T(2,128)}, u32[]{:S(2)}) copy-start(f32[1,2,4,128]{3,1,2,0:T(2,128)} %copy-done.44) | copy-start | bytes 12292
  799.9 36.2 %copy-start.48 = (f32[256]{0:T(256)S(1)}, f32[256]{0:T(256)}, u32[]{:S(2)}) copy-start(f32[256]{0:T(256)} %copy-done.47) | copy-start | bytes 3076
  800.9 76.9 %copy-start.50 = (f32[256]{0:T(256)S(1)}, f32[256]{0:T(256)}, u32[]{:S(2)}) copy-start(f32[256]{0:T(256)} %copy-done.49) | copy-start | bytes 3076
  800.9 76.9 %copy-start.8 = (bf16[256,1024]{1,0:T(8,128)(2,1)S(1)}, bf16[256,1024]{1,0:T(8,128)(2,1)}, u32[]{:S(2)}) copy-start(bf16[256,1024]{1,0:T(8,128)(2,1)} %reduce-scatter.5.cloned.1.call-done) | copy-start | bytes 1572868
  800.9 76.9 %copy-start.13 = (bf16[1,256,1024]{2,1,0:T(8,128)(2,1)S(1)}, bf16[1,256,1024]{2,1,0:T(8,128)(2,1)}, u32[]{:S(2)}) copy-start(bf16[1,256,1024]{2,1,0:T(8,128)(2,1)} %param.18) | copy-start | bytes 1572868
  800.9 255.9 %all-to-all-start.8 = ((bf16[4,256,768]{2,1,0:T(8,128)(2,1)}), bf16[4,256,768]{2,1,0:T(8,128)(2,1)}, u32[]{:S(2)}, u32[]{:S(2)}) async-start(bf16[4,256,768]{2,1,0:T(8,128)(2,1)} %bitcast.246), calls=%async_computation.12 | async-start | bytes 3145728 | tf_op jit(solution)/shard_map/all_to_all | solution.py:58
  1056.7 324.5 %all-to-all-start.9 = ((bf16[4,256,768]{2,1,0:T(8,128)(2,1)}), bf16[4,256,768]{2,1,0:T(8,128)(2,1)}, u32[]{:S(2)}, u32[]{:S(2)}) async-start(bf16[4,256,768]{2,1,0:T(8,128)(2,1)} %bitcast.247), calls=%async_computation.13 | async-start | bytes 3145728 | tf_op jit(solution)/shard_map/all_to_all | solution.py:58
  (53 other events, 287.0 us)
Sparse Core Ops, SparseCore 0:
  22.3 26.2 all-gather.19
  112.0 31.7 reduce-scatter.4
  147.3 33.7 all-gather.21
  183.2 33.8 all-gather.23
  245.9 31.4 reduce-scatter.8
  281.8 22.5 all-gather.25
  341.6 73.3 all-gather.29
  417.1 71.6 all-gather.31
  491.5 123.1 all-gather.27
  617.3 174.6 all-gather.35
  795.1 40.9 reduce-scatter.10
  839.2 30.3 reduce-scatter.6
  872.3 176.4 all-gather.37
  1050.8 123.1 all-gather.33
  1176.0 174.6 all-gather.39
